TPU v7x, 32 devices: a whole 2x2x4 slice. The times are simulated.
32 devices in a mesh: row: 16 (over z, y, core), col: 2 (over x).
Axes of the slice: x: 2, y: 2, z: 4, core: 2. Of those that a mesh axis runs over, the one named last changes fastest.
Arguments:
- source: float32 [4096, 2048], P('row', 'col'), may hold values from 0.25 to 4
- boxes_a: float32 [16, 8, 512, 512], P('row', 'col'), may hold values from 0.25 to 4
- shifts_a: int32 [16, 8, 2], P('row', 'col'), may hold values from -128 to -1
- widths_a: int32 [16, 8, 2], P('row', 'col'), may hold values from 256 to 512
- boxes_b: float32 [16, 8, 512, 512], P('row', 'col'), may hold values from 0.25 to 4
- shifts_b: int32 [16, 8, 2], P('row', 'col'), may hold values from -128 to -1
- widths_b: int32 [16, 8, 2], P('row', 'col'), may hold values from 256 to 512
Outputs:
- smoothed: float32 [4096, 2048], P('row', 'col')
Inputs may be any that keep to these rules, and one draw needn't show every extreme that they name: `shifts_a`: first entry: rows, second: columns. `widths_a`: first entry: rows, second: columns. `shifts_b`: first entry: rows, second: columns. `widths_b`: first entry: rows, second: columns.
All inputs are finite; a program needn't handle non-finite values.
Results may differ from a plain program's by a relative error of at most 0.0003.
Values sent between devices are 32-bit elements; how exact they have to be, the bound alone decides.
A program may use at most 64 MiB of HBM per device.

v0:
```python
import math

import jax
import jax.numpy as jnp
from jax import lax
from jax.sharding import PartitionSpec as P

S = 256
BOX = 512
ITERS = 3
RADIUS = 8


kernel_eps = 0.05
blur_sigma = 2.0


def from_behind(array, axis, by):
    length = lax.axis_size(axis)
    return lax.ppermute(array, axis, [(i, (i + by) % length) for i in range(length)])


def padded_2(cells, sides, width):
    for axis, dim in sides:
        count = lax.axis_size(axis)
        head = lax.slice_in_dim(cells, 0, width, axis=dim)
        tail = lax.slice_in_dim(cells, cells.shape[dim] - width, cells.shape[dim], axis=dim)
        cells = jnp.concatenate(
            [
                lax.ppermute(tail, axis, [(i, (i + 1) % count) for i in range(count)]),
                cells,
                lax.ppermute(head, axis, [((i + 1) % count, i) for i in range(count)]),
            ],
            axis=dim,
        )
    return cells


def table(patch_displacement):
    rows = jnp.arange(S, dtype=jnp.int32)
    cols = jnp.arange(BOX, dtype=jnp.int32)
    dist = (patch_displacement + cols[None, :] - rows[:, None]).astype(jnp.float32) / S
    return jnp.exp(-dist * dist / kernel_eps).astype(jnp.bfloat16)


def masked(patch_rectangle, patch_extent):
    index = jnp.arange(BOX, dtype=jnp.int32)
    keep_rows = (index < patch_extent[0]).astype(jnp.float32)
    keep_cols = (index < patch_extent[1]).astype(jnp.float32)
    return patch_rectangle * keep_rows[:, None] * keep_cols[None, :]


def apply_back(horizontal_kernel_grid, vertical_kernel_grid, multiplier_array):
    inner = lax.dot_general(
        horizontal_kernel_grid,
        multiplier_array.astype(jnp.bfloat16),
        (((0,), (0,)), ((), ())),
        preferred_element_type=jnp.float32,
    )
    return jnp.dot(
        inner.astype(jnp.bfloat16), vertical_kernel_grid, preferred_element_type=jnp.float32
    )


def apply_fwd(horizontal_kernel_grid, vertical_kernel_grid, multiplier_array):
    inner = jnp.dot(
        horizontal_kernel_grid,
        multiplier_array.astype(jnp.bfloat16),
        preferred_element_type=jnp.float32,
    )
    return lax.dot_general(
        inner.astype(jnp.bfloat16),
        vertical_kernel_grid,
        (((1,), (1,)), ((), ())),
        preferred_element_type=jnp.float32,
    )


def entropic_transport_iterate(
    probability_measure, patch_rectangle, patch_displacement, patch_extent, initial_corner_index
):
    horizontal_kernel_grid = table(patch_displacement[0])
    vertical_kernel_grid = table(patch_displacement[1])
    target = masked(patch_rectangle, patch_extent)
    multiplier_array = initial_corner_index
    lagrange_multiplier_field = target
    for step in range(ITERS):
        lagrange_multiplier_field = target / apply_back(
            horizontal_kernel_grid, vertical_kernel_grid, multiplier_array
        )
        multiplier_array = probability_measure / apply_fwd(
            horizontal_kernel_grid, vertical_kernel_grid, lagrange_multiplier_field
        )
    return (
        multiplier_array,
        lagrange_multiplier_field,
        horizontal_kernel_grid,
        vertical_kernel_grid,
    )


def section_first(probability_measure, patch_rectangle, patch_displacement, patch_extent):
    multiplier_array, lagrange_multiplier_field, horizontal_kernel_grid, vertical_kernel_grid = (
        entropic_transport_iterate(
            probability_measure,
            patch_rectangle,
            patch_displacement,
            patch_extent,
            jnp.ones_like(probability_measure),
        )
    )
    return multiplier_array


def section_second(
    probability_measure, initial_corner_index, patch_rectangle, patch_displacement, patch_extent
):
    multiplier_array, lagrange_multiplier_field, horizontal_kernel_grid, vertical_kernel_grid = (
        entropic_transport_iterate(
            probability_measure,
            patch_rectangle,
            patch_displacement,
            patch_extent,
            initial_corner_index,
        )
    )
    return lagrange_multiplier_field * apply_back(
        horizontal_kernel_grid, vertical_kernel_grid, multiplier_array
    )


def blur_pairs():
    raw = [
        math.exp(-(step * step) / (2.0 * blur_sigma * blur_sigma))
        for step in range(-RADIUS, RADIUS + 1)
    ]
    total = sum(raw)
    return [(step, raw[step + RADIUS] / total) for step in range(-RADIUS, RADIUS + 1)]


def margin_blur(padded, axis):
    length = padded.shape[axis] - 2 * RADIUS
    result = None
    for step, weight in blur_pairs():
        piece = weight * lax.slice_in_dim(padded, RADIUS + step, RADIUS + step + length, axis=axis)
        result = piece if result is None else result + piece
    return result


def split_cells(field, per_dev):
    return field.reshape(S, per_dev, S).transpose(1, 0, 2)


def on_device(source, boxes_a, shifts_a, widths_a, boxes_b, shifts_b, widths_b):
    cols_here = source.shape[1]
    per_dev = cols_here // S
    half = S // 2
    first = jax.vmap(section_first)(
        split_cells(source, per_dev), boxes_a[0], shifts_a[0], widths_a[0]
    )
    u_field = first.transpose(1, 0, 2).reshape(S, cols_here)
    stacked = jnp.stack([u_field, source])
    below = from_behind(stacked[:, :half], "row", -1)
    rowset = jnp.concatenate([stacked[:, half:], below], axis=1)
    beside = from_behind(rowset[:, :, :half], "col", -1)
    moved = jnp.concatenate([rowset[:, :, half:], beside], axis=2)
    plans = jax.vmap(section_second)(
        split_cells(moved[1], per_dev),
        split_cells(moved[0], per_dev),
        boxes_b[0],
        shifts_b[0],
        widths_b[0],
    )
    canvas = jnp.zeros((3 * S, cols_here + 2 * S), jnp.float32)

    def place(index, canvas):
        top = half + shifts_b[0, index, 0]
        left = index * S + half + shifts_b[0, index, 1]
        region = lax.dynamic_slice(canvas, (top, left), (BOX, BOX))
        return lax.dynamic_update_slice(canvas, region + plans[index], (top, left))

    canvas = lax.fori_loop(0, per_dev, place, canvas)
    summed = canvas[:S]
    for step in (1, 2):
        summed = summed + from_behind(canvas[step * S : (step + 1) * S], "row", step)
    extra = from_behind(summed[:, cols_here:], "col", 1)
    gathered = summed[:, :cols_here].at[:, : 2 * S].add(extra)
    padded = padded_2(gathered, (("row", 0),), RADIUS)
    row_smooth = margin_blur(padded, 0)
    padded = padded_2(row_smooth, (("col", 1),), RADIUS)
    return margin_blur(padded, 1)


def solution(mesh):
    return jax.shard_map(
        on_device,
        mesh=mesh,
        in_specs=(
            P("row", "col"),
            P("row", "col", None, None),
            P("row", "col", None),
            P("row", "col", None),
            P("row", "col", None, None),
            P("row", "col", None),
            P("row", "col", None),
        ),
        out_specs=P("row", "col"),
        check_vma=False,
    )
```

profile of v0, /device:TPU:1, one launch (start us, length us, event | category | flops | bytes accessed | tf_op | source)
XLA Modules:
  0.0 229.7 jit_solution(5828483001850037112)
XLA Ops:
  0.8 1.0 convolution_convert_fusion
  2.5 5.6 %fusion.37 = bf16[4,256,512]{2,1,0:T(8,128)(2,1)} fusion(f32[1,4,512,512]{3,2,1,0:T(8,128)} %param.12, f32[4,512]{1,0:T(4,128)S(1)} %get-tuple-element.159, f32[4,512]{1,0:T(4,128)S(1)} %get-tuple-element.158, bf16[4,512,256]{2,1,0:T(8,128)(2,1)S(1)} %convolution_convert_fusion, s32[4,512]{1,0:T(4,128)S(1)} %get-tuple-element.160, ...), kind=kOutput, calls=%fused_computation.82 | convolution fusion | flops 1085800448 | bytes 6324224 | tf_op jit(solution)/shard_map/vmap()/dot_general | solution.py:66
  8.0 2.9 %convolution_convert_fusion.6 = bf16[4,512,256]{2,1,0:T(8,128)(2,1)S(1)} fusion(f32[4,256,256]{1,2,0:T(8,128)S(1)} %bitcast.99, bf16[4,256,512]{2,1,0:T(8,128)(2,1)} %fusion.37, s32[4,512]{1,0:T(4,128)S(1)} %get-tuple-element.160, s32[4,512]{1,0:T(4,128)S(1)} %get-tuple-element.161), kind=kOutput, calls=%fused_computation.90 | convolution fusion | flops 545259520 | bytes 3162112 | tf_op jit(solution)/shard_map/vmap()/dot_general | solution.py:54
  10.9 5.5 %fusion.36 = bf16[4,256,512]{2,1,0:T(8,128)(2,1)} fusion(f32[1,4,512,512]{3,2,1,0:T(8,128)} %param.12, f32[4,512]{1,0:T(4,128)S(1)} %get-tuple-element.159, f32[4,512]{1,0:T(4,128)S(1)} %get-tuple-element.158, bf16[4,512,256]{2,1,0:T(8,128)(2,1)S(1)} %convolution_convert_fusion.6, s32[4,512]{1,0:T(4,128)S(1)} %get-tuple-element.160, ...), kind=kOutput, calls=%fused_computation.81 | convolution fusion | flops 1085800448 | bytes 6324224 | tf_op jit(solution)/shard_map/vmap()/dot_general | solution.py:66
  16.4 3.9 %convolution_convert_fusion.5 = bf16[4,512,256]{2,1,0:T(8,128)(2,1)} fusion(f32[4,256,256]{1,2,0:T(8,128)S(1)} %bitcast.100, bf16[4,256,512]{2,1,0:T(8,128)(2,1)} %fusion.36, s32[4,512]{1,0:T(4,128)S(1)} %get-tuple-element.160, s32[4,512]{1,0:T(4,128)S(1)} %get-tuple-element.161), kind=kOutput, calls=%fused_computation.89 | convolution fusion | flops 545259520 | bytes 3162112 | tf_op jit(solution)/shard_map/vmap()/dot_general | solution.py:54
  20.3 4.9 %fusion.35 = bf16[4,256,512]{2,1,0:T(8,128)(2,1)S(1)} fusion(f32[1,4,512,512]{3,2,1,0:T(8,128)} %param.12, f32[4,512]{1,0:T(4,128)S(1)} %get-tuple-element.159, f32[4,512]{1,0:T(4,128)S(1)} %get-tuple-element.158, bf16[4,512,256]{2,1,0:T(8,128)(2,1)} %convolution_convert_fusion.5, s32[4,512]{1,0:T(4,128)S(1)} %get-tuple-element.160, ...), kind=kOutput, calls=%fused_computation.80 | convolution fusion | flops 1085800448 | bytes 6324224 | tf_op jit(solution)/shard_map/vmap()/dot_general | solution.py:66
  25.2 2.0 fusion.44
  27.1 1.6 copy.9
  29.5 14.8 %collective-permute-done = f32[2,128,1024]{2,1,0:T(8,128)} collective-permute-done((f32[2,128,1024]{2,1,0:T(8,128)S(1)}, f32[2,128,1024]{2,1,0:T(8,128)}, u32[]{:S(2)}, u32[]{:S(2)}) %collective-permute-start) | collective-permute-done | bytes 1048608 | tf_op jit(solution)/shard_map/ppermute | solution.py:20
  44.2 0.9 pad_maximum_fusion.6
  45.2 1.3 collective-permute-start.1
  46.5 1.3 fusion.32
  47.8 2.6 %collective-permute-done.1 = f32[2,256,128]{2,1,0:T(8,128)S(1)} collective-permute-done((f32[2,256,128]{2,1,0:T(8,128)S(1)}, f32[2,256,128]{2,1,0:T(8,128)S(1)}, u32[]{:S(2)}, u32[]{:S(2)}) %collective-permute-start.1) | collective-permute-done | bytes 262176 | tf_op jit(solution)/shard_map/ppermute | solution.py:20
  50.4 1.1 fusion.91
  51.5 1.7 reshape_squeeze.4
  53.2 1.0 fusion.141
  54.6 0.9 convolution_convert_fusion.4
  55.6 4.5 %fusion.34 = bf16[4,256,512]{2,1,0:T(8,128)(2,1)S(1)} fusion(f32[1,4,512,512]{3,2,1,0:T(8,128)} %param.15, f32[4,512]{1,0:T(4,128)S(1)} %get-tuple-element.155, f32[4,512]{1,0:T(4,128)S(1)} %get-tuple-element.154, bf16[4,512,256]{2,1,0:T(8,128)(2,1)S(1)} %convolution_convert_fusion.4, s32[4,512]{1,0:T(4,128)S(1)} %get-tuple-element.156, ...), kind=kOutput, calls=%fused_computation.79 | convolution fusion | flops 1085800448 | bytes 6324224 | tf_op jit(solution)/shard_map/vmap()/dot_general | solution.py:66
  60.1 0.9 fusion.149
  61.8 0.9 convolution_convert_fusion.3
  62.8 4.5 %fusion.33 = bf16[4,256,512]{2,1,0:T(8,128)(2,1)S(1)} fusion(f32[1,4,512,512]{3,2,1,0:T(8,128)} %param.15, f32[4,512]{1,0:T(4,128)S(1)} %get-tuple-element.155, f32[4,512]{1,0:T(4,128)S(1)} %get-tuple-element.154, bf16[4,512,256]{2,1,0:T(8,128)(2,1)S(1)} %convolution_convert_fusion.3, s32[4,512]{1,0:T(4,128)S(1)} %get-tuple-element.156, ...), kind=kOutput, calls=%fused_computation.78 | convolution fusion | flops 1085800448 | bytes 6324224 | tf_op jit(solution)/shard_map/vmap()/dot_general | solution.py:66
  69.0 5.3 %fusion.2 = f32[4,512,512]{2,1,0:T(8,128)} fusion(f32[1,4,512,512]{3,2,1,0:T(8,128)} %param.15, f32[4,512]{1,0:T(4,128)S(1)} %get-tuple-element.155, f32[4,512]{1,0:T(4,128)S(1)} %get-tuple-element.154, s32[4,512]{1,0:T(4,128)S(1)} %get-tuple-element.156, s32[4,512]{1,0:T(4,128)S(1)} %get-tuple-element.157, bf16[4,256,256]{2,0,1:T(4,128)(2,1)S(1)} %fusion.181), kind=kOutput, calls=%fused_computation.40 | convolution fusion | flops 816316416 | bytes 8945664 | tf_op jit(solution)/shard_map/vmap()/dot_general | solution.py:60
  74.3 3.9 %fusion.42 = f32[4,256,256]{2,1,0:T(8,128)S(1)} fusion(f32[4,512,512]{2,1,0:T(8,128)} %fusion.2, s32[4,512]{1,0:T(4,128)S(1)} %get-tuple-element.156, s32[4,512]{1,0:T(4,128)S(1)} %get-tuple-element.157), kind=kOutput, calls=%fused_computation.91 | convolution fusion | flops 814219264 | bytes 5259264 | tf_op jit(solution)/shard_map/vmap()/dot_general | solution.py:71
  78.9 6.0 %convolution_multiply_fusion = f32[4,512,512]{2,1,0:T(8,128)} fusion(f32[4,512,512]{2,1,0:T(8,128)} %fusion.2, s32[4,512]{1,0:T(4,128)S(1)} %get-tuple-element.156, s32[4,512]{1,0:T(4,128)S(1)} %get-tuple-element.157, bf16[4,256,256]{2,0,1:T(4,128)(2,1)S(1)} %fusion.182), kind=kOutput, calls=%fused_computation.45 | convolution fusion | flops 814219264 | bytes 8929280 | tf_op jit(solution)/shard_map/vmap()/dot_general | solution.py:60
  85.0 2.7 %broadcast_in_dim.2 = f32[768,1536]{1,0:T(8,128)} broadcast(f32[]{:T(128)} %constant.124.clone.1), dimensions={} | broadcast | bytes 4718596 | tf_op jit(solution)/shard_map/broadcast_in_dim | solution.py:174
  87.7 49.2 %while.16 = (s32[]{:T(128)}, f32[768,1536]{1,0:T(8,128)}, s32[1,4,2]{1,2,0:T(2,128)S(1)}, f32[4,512,512]{2,1,0:T(8,128)}, s32[]{:T(128)}, /*index=5*/s32[1,1,1]{...) while((s32[]{:T(128)}, f32[768,1536]{1,0:T(8,128)}, ...), condition=%wide.region_1.0_spmd, body=%wide.region_0.0_spmd.sunk | while | flops 262156 | bytes 5243141 | solution.py:182
  90.4 2.0 bitcast_add_fusion.2
  92.4 7.9 %dynamic_update_slice.11 = f32[768,1536]{1,0:T(8,128)} dynamic-update-slice(f32[768,1536]{1,0:T(8,128)} %get-tuple-element.203, f32[512,512]{1,0:T(8,128)S(1)} %bitcast_add_fusion.2, s32[]{:T(128)S(6)} %select_n.34, s32[]{:T(128)S(6)} %select_n.35) | dynamic-update-slice | bytes 2097156 | tf_op jit(solution)/shard_map/while/body/eval_jaxpr/dynamic_update_slice | solution.py:180
  103.0 2.0 bitcast_add_fusion.2
  105.0 7.8 %dynamic_update_slice.11 = f32[768,1536]{1,0:T(8,128)} dynamic-update-slice(f32[768,1536]{1,0:T(8,128)} %get-tuple-element.203, f32[512,512]{1,0:T(8,128)S(1)} %bitcast_add_fusion.2, s32[]{:T(128)S(6)} %select_n.34, s32[]{:T(128)S(6)} %select_n.35) | dynamic-update-slice | bytes 2097156 | tf_op jit(solution)/shard_map/while/body/eval_jaxpr/dynamic_update_slice | solution.py:180
  115.5 2.0 bitcast_add_fusion.2
  117.5 7.8 %dynamic_update_slice.11 = f32[768,1536]{1,0:T(8,128)} dynamic-update-slice(f32[768,1536]{1,0:T(8,128)} %get-tuple-element.203, f32[512,512]{1,0:T(8,128)S(1)} %bitcast_add_fusion.2, s32[]{:T(128)S(6)} %select_n.34, s32[]{:T(128)S(6)} %select_n.35) | dynamic-update-slice | bytes 2097156 | tf_op jit(solution)/shard_map/while/body/eval_jaxpr/dynamic_update_slice | solution.py:180
  128.0 2.0 bitcast_add_fusion.2
  130.0 6.9 %dynamic_update_slice.11 = f32[768,1536]{1,0:T(8,128)} dynamic-update-slice(f32[768,1536]{1,0:T(8,128)} %get-tuple-element.203, f32[512,512]{1,0:T(8,128)S(1)} %bitcast_add_fusion.2, s32[]{:T(128)S(6)} %select_n.34, s32[]{:T(128)S(6)} %select_n.35) | dynamic-update-slice | bytes 2097156 | tf_op jit(solution)/shard_map/while/body/eval_jaxpr/dynamic_update_slice | solution.py:180
  136.9 2.1 fusion.248
  139.0 2.7 %collective-permute-start.2 = (f32[256,1536]{1,0:T(8,128)S(1)}, f32[256,1536]{1,0:T(8,128)S(1)}, u32[]{:S(2)}, u32[]{:S(2)}) collective-permute-start(f32[256,1536]{1,0:T(8,128)S(1)} %get-tuple-element.138), channel_id=1, source_target_pairs={{0,2},{2,4},{4,6},{6,8},{8,10},{10,12},{12,14},{14,16},{16,18},{18... | collective-permute-start | bytes 4718600 | tf_op jit(solution)/shard_map/ppermute | solution.py:20
  141.8 2.9 %collective-permute-start.3 = (f32[256,1536]{1,0:T(8,128)S(1)}, f32[256,1536]{1,0:T(8,128)S(1)}, u32[]{:S(2)}, u32[]{:S(2)}) collective-permute-start(f32[256,1536]{1,0:T(8,128)S(1)} %get-tuple-element.139), channel_id=1, source_target_pairs={{0,4},{2,6},{4,8},{6,10},{8,12},{10,14},{12,16},{14,18},{16,20},{1... | collective-permute-start | bytes 4718600 | tf_op jit(solution)/shard_map/ppermute | solution.py:20
  144.7 29.1 %collective-permute-done.2 = f32[256,1536]{1,0:T(8,128)S(1)} collective-permute-done((f32[256,1536]{1,0:T(8,128)S(1)}, f32[256,1536]{1,0:T(8,128)S(1)}, u32[]{:S(2)}, u32[]{:S(2)}) %collective-permute-start.2) | collective-permute-done | bytes 1572896 | tf_op jit(solution)/shard_map/ppermute | solution.py:20
  173.8 25.3 %collective-permute-done.3 = f32[256,1536]{1,0:T(8,128)S(1)} collective-permute-done((f32[256,1536]{1,0:T(8,128)S(1)}, f32[256,1536]{1,0:T(8,128)S(1)}, u32[]{:S(2)}, u32[]{:S(2)}) %collective-permute-start.3) | collective-permute-done | bytes 1572896 | tf_op jit(solution)/shard_map/ppermute | solution.py:20
  199.1 1.8 add_add_fusion
  200.9 1.2 collective-permute-start.4
  202.9 6.2 %collective-permute-done.4 = f32[256,512]{1,0:T(8,128)S(1)} collective-permute-done((f32[256,512]{1,0:T(8,128)S(1)}, f32[256,512]{1,0:T(8,128)S(1)}, u32[]{:S(2)}, u32[]{:S(2)}) %collective-permute-start.4) | collective-permute-done | bytes 524320 | tf_op jit(solution)/shard_map/ppermute | solution.py:20
  211.0 2.2 collective-permute-done.6
  213.2 2.4 %fusion.96 = f32[256,1024]{1,0:T(8,128)S(1)} fusion(f32[8,1024]{1,0:T(8,128)S(1)} %collective-permute-done.6, f32[8,1024]{1,0:T(8,128)S(1)} %collective-permute-done.5, f32[256,1024]{1,0:T(8,128)S(1)} %fusion.183), kind=kLoop, calls=%fused_computation.161 | loop fusion | flops 12845056 | bytes 2162688 | tf_op jit(solution)/shard_map/add | solution.py:146
  215.7 1.2 collective-permute-start.7
  217.2 4.0 %collective-permute-done.7 = f32[256,8]{1,0:T(8,128)S(1)} collective-permute-done((f32[256,8]{1,0:T(8,128)S(1)}, f32[256,8]{1,0:T(8,128)S(1)}, u32[]{:S(2)}, u32[]{:S(2)}) %collective-permute-start.7) | collective-permute-done | bytes 8224 | tf_op jit(solution)/shard_map/ppermute | solution.py:30
  221.3 1.7 collective-permute-done.8
  223.0 6.7 %fusion.50 = f32[256,1024]{1,0:T(8,128)} fusion(f32[256,1024]{1,0:T(8,128)S(1)} %fusion.96, f32[256,8]{1,0:T(8,128)S(1)} %collective-permute-done.8, f32[256,8]{1,0:T(8,128)S(1)} %collective-permute-done.7), kind=kLoop, calls=%fused_computation.115 | loop fusion | flops 12845056 | bytes 2113536 | tf_op jit(solution)/shard_map/add | solution.py:146
  (40 shorter events, 11.9 us)
Async XLA Ops:
  0.8 1.0 copy-start.3
  0.8 1.2 copy-start
  28.7 0.7 copy-start.2
  28.7 0.7 copy-start.4
  28.9 15.3 %collective-permute-start = (f32[2,128,1024]{2,1,0:T(8,128)S(1)}, f32[2,128,1024]{2,1,0:T(8,128)}, u32[]{:S(2)}, u32[]{:S(2)}) collective-permute-start(f32[2,128,1024]{2,1,0:T(8,128)S(1)} %get-tuple-element.141), channel_id=1, source_target_pairs={{0,30},{2,0},{4,2},{6,4},{8,6},{10,8},{12,10},{14,12},{16,14},{18,... | collective-permute-start | bytes 3145736 | tf_op jit(solution)/shard_map/ppermute | solution.py:20
  45.2 5.3 %collective-permute-start.1 = (f32[2,256,128]{2,1,0:T(8,128)S(1)}, f32[2,256,128]{2,1,0:T(8,128)S(1)}, u32[]{:S(2)}, u32[]{:S(2)}) collective-permute-start(f32[2,256,128]{2,1,0:T(8,128)S(1)} %pad_maximum_fusion.6), channel_id=1, source_target_pairs={{0,1},{1,0},{2,3},{3,2},{4,5},{5,4},{6,7},{7,6},{8,9},{9,8},{10,11... | collective-permute-start | bytes 786440 | tf_op jit(solution)/shard_map/ppermute | solution.py:20
  50.4 1.1 copy-start.1
  139.0 34.8 %collective-permute-start.2 = (f32[256,1536]{1,0:T(8,128)S(1)}, f32[256,1536]{1,0:T(8,128)S(1)}, u32[]{:S(2)}, u32[]{:S(2)}) collective-permute-start(f32[256,1536]{1,0:T(8,128)S(1)} %get-tuple-element.138), channel_id=1, source_target_pairs={{0,2},{2,4},{4,6},{6,8},{8,10},{10,12},{12,14},{14,16},{16,18},{18... | collective-permute-start | bytes 4718600 | tf_op jit(solution)/shard_map/ppermute | solution.py:20
  141.8 57.3 %collective-permute-start.3 = (f32[256,1536]{1,0:T(8,128)S(1)}, f32[256,1536]{1,0:T(8,128)S(1)}, u32[]{:S(2)}, u32[]{:S(2)}) collective-permute-start(f32[256,1536]{1,0:T(8,128)S(1)} %get-tuple-element.139), channel_id=1, source_target_pairs={{0,4},{2,6},{4,8},{6,10},{8,12},{10,14},{12,16},{14,18},{16,20},{1... | collective-permute-start | bytes 4718600 | tf_op jit(solution)/shard_map/ppermute | solution.py:20
  200.9 8.1 %collective-permute-start.4 = (f32[256,512]{1,0:T(8,128)S(1)}, f32[256,512]{1,0:T(8,128)S(1)}, u32[]{:S(2)}, u32[]{:S(2)}) collective-permute-start(f32[256,512]{1,0:T(8,128)S(1)} %slice.288), channel_id=1, source_target_pairs={{0,1},{1,0},{2,3},{3,2},{4,5},{5,4},{6,7},{7,6},{8,9},{9,8},{10,11... | collective-permute-start | bytes 1572872 | tf_op jit(solution)/shard_map/ppermute | solution.py:20
  209.8 1.3 collective-permute-start.5
  209.8 3.4 %collective-permute-start.6 = (f32[8,1024]{1,0:T(8,128)S(1)}, f32[8,1024]{1,0:T(8,128)S(1)}, u32[]{:S(2)}, u32[]{:S(2)}) collective-permute-start(f32[8,1024]{1,0:T(8,128)S(1)} %get-tuple-element.145), channel_id=1, source_target_pairs={{2,0},{4,2},{6,4},{8,6},{10,8},{12,10},{14,12},{16,14},{18,16},{20... | collective-permute-start | bytes 98312 | tf_op jit(solution)/shard_map/ppermute | solution.py:32
  215.7 5.6 %collective-permute-start.7 = (f32[256,8]{1,0:T(8,128)S(1)}, f32[256,8]{1,0:T(8,128)S(1)}, u32[]{:S(2)}, u32[]{:S(2)}) collective-permute-start(f32[256,8]{1,0:T(8,128)S(1)} %get-tuple-element.142), channel_id=1, source_target_pairs={{0,1},{1,0},{2,3},{3,2},{4,5},{5,4},{6,7},{7,6},{8,9},{9,8},{10,11... | collective-permute-start | bytes 24584 | tf_op jit(solution)/shard_map/ppermute | solution.py:30
  216.9 6.1 %collective-permute-start.8 = (f32[256,8]{1,0:T(8,128)S(1)}, f32[256,8]{1,0:T(8,128)S(1)}, u32[]{:S(2)}, u32[]{:S(2)}) collective-permute-start(f32[256,8]{1,0:T(8,128)S(1)} %get-tuple-element.143), channel_id=1, source_target_pairs={{1,0},{0,1},{3,2},{2,3},{5,4},{4,5},{7,6},{6,7},{9,8},{8,9},{11,10... | collective-permute-start | bytes 24584 | tf_op jit(solution)/shard_map/ppermute | solution.py:32
where the time goes:
time: 231 us; the launch traced here: 230 us
  waiting for transfers between devices  86.6 us (37%)
  matrix products  53.4 us (23%)
  local copies, waits for them, and re-layouts  43.5 us (19%)
  other arithmetic  27.5 us (12%)
  starting transfers between devices  10.3 us (4%)
  loops' own time  8.16 us (4%)
    ppermute x5, waiting for transfers between devices, from_behind(): lax.ppermute(array, axis, [(i, (i + by) % length) for i in range(length)])  78 us
    dynamic_update_slice x4, local copies, waits for them, and re-layouts, place(): return lax.dynamic_update_slice(canvas, region + plans[index], (top, left))  30.4 us
    dot_general x5, matrix products, apply_fwd(): jnp.dot(horizontal_kernel_grid, multiplier_array.astype(jnp.bfloat16), pr...  25 us
    dot_general x2, matrix products, apply_back(): jnp.dot(inner.astype(jnp.bfloat16), vertical_kernel_grid, preferred_eleme...  11.3 us
    dot_general x5, matrix products, apply_back(): lax.dot_general(horizontal_kernel_grid, multiplier_array.astype(jnp.bfloa...  9.6 us
    add x2, other arithmetic, margin_blur(): result = piece if result is None else result + piece  9.07 us
    ppermute x5, starting transfers between devices, from_behind(): lax.ppermute(array, axis, [(i, (i + by) % length) for i in range(length)])  8.21 us
    another operation x1, loops' own time, on_device(): canvas = lax.fori_loop(0, per_dev, place, canvas)  8.16 us
  transfers between devices with their start and end apart: 9, of which 9 were waited for; matrix products, arithmetic and copies ran while one was open for 1% of the time, Pallas kernels for 0%

commit v1 on v0

v1 whole, which is shorter than its diff:
```python
import functools
import math

import jax
import jax.numpy as jnp
from jax import lax
from jax.experimental import pallas as pl
from jax.experimental.pallas import tpu as pltpu
from jax.sharding import PartitionSpec as P

S = 256
BOX = 512
ITERS = 3
RADIUS = 8
LANES = 128
HALF = S // 2
DOWN2 = HALF + RADIUS
TALL = RADIUS + 2 * S + DOWN2

kernel_eps = 0.05
blur_sigma = 2.0
blur_total = sum(
    math.exp(-(d * d) / (2.0 * blur_sigma * blur_sigma)) for d in range(-RADIUS, RADIUS + 1)
)


def gauss(offset, shape, box_dim):
    k = lax.broadcasted_iota(jnp.int32, shape, box_dim)
    p = lax.broadcasted_iota(jnp.int32, shape, 1 - box_dim)
    dist = (offset + k - p).astype(jnp.float32) * (1.0 / S)
    return jnp.exp(dist * dist * (-1.0 / kernel_eps)).astype(jnp.bfloat16)


def blur_weight(d):
    f = d.astype(jnp.float32)
    w = jnp.exp(f * f * (-1.0 / (2.0 * blur_sigma * blur_sigma))) * (1.0 / blur_total)
    return jnp.where(jnp.abs(d) <= RADIUS, w, 0.0)


def split(x):
    hi = x.astype(jnp.bfloat16)
    return hi, (x - hi.astype(jnp.float32)).astype(jnp.bfloat16)


def dot(a, b):
    return jnp.dot(a, b, preferred_element_type=jnp.float32)


def dot_t(a, b):
    return lax.dot_general(a, b, (((1,), (1,)), ((), ())), preferred_element_type=jnp.float32)


def dot_split(a, b):
    (ah, al), (bh, bl) = a, b
    return dot(ah, bh) + (dot(ah, bl) + dot(al, bh))


def bf(x):
    return x.astype(jnp.bfloat16)


def target_of(box_ref, height, width):
    rows = lax.broadcasted_iota(jnp.int32, (BOX, BOX), 0)
    cols = lax.broadcasted_iota(jnp.int32, (BOX, BOX), 1)
    return jnp.where((rows < height) & (cols < width), box_ref[0, 0], 0.0)


def kernel_a(shift_ref, width_ref, a_ref, box_ref, u_ref, tgt):
    j = pl.program_id(0)
    o_r, o_c = shift_ref[j, 0], shift_ref[j, 1]
    kr = gauss(o_r, (S, BOX), 1)
    krt = gauss(o_r, (BOX, S), 0)
    kc = gauss(o_c, (S, BOX), 1)
    tgt[...] = target_of(box_ref, width_ref[j, 0], width_ref[j, 1])
    a = a_ref[...]
    in_r = bf(jnp.sum(krt.astype(jnp.float32), axis=1, keepdims=True)).astype(jnp.float32)
    in_c = jnp.sum(kc.astype(jnp.float32), axis=0, keepdims=True)
    back = in_r * in_c
    for step in range(ITERS):
        v = bf(tgt[...] / back)
        u = a / dot_t(bf(dot(kr, v)), kc)
        if step < ITERS - 1:
            back = dot(bf(dot(krt, bf(u))), kc)
    u_ref[...] = u


def kernel_b(per_dev, shift_ref, width_ref, a_ref, u_ref, box_ref, up_ref, own_ref, d1_ref, d2_ref, tgt, canvas):
    j = pl.program_id(0)
    o_r, o_c = shift_ref[j, 0], shift_ref[j, 1]
    wide = canvas.shape[1]

    @pl.when(j == 0)
    def _():
        canvas[...] = jnp.zeros_like(canvas)

    kr = gauss(o_r, (S, BOX), 1)
    krt = gauss(o_r, (BOX, S), 0)
    kc = gauss(o_c, (S, BOX), 1)
    tgt[...] = target_of(box_ref, width_ref[j, 0], width_ref[j, 1])
    a = a_ref[...]
    u = u_ref[...]
    for step in range(ITERS):
        back = dot(bf(dot(krt, bf(u))), kc)
        v = tgt[...] / back
        u = a / dot_t(bf(dot(kr, bf(v))), kc)
    plan = v * dot(bf(dot(krt, bf(u))), kc)

    y = lax.broadcasted_iota(jnp.int32, (TALL, BOX), 0) - RADIUS
    k = lax.broadcasted_iota(jnp.int32, (TALL, BOX), 1)
    rowed = dot_split(split(blur_weight(HALF + o_r + k - y)), split(plan))
    s = HALF + o_c
    lane = lax.broadcasted_iota(jnp.int32, (TALL, LANES), 1)
    turned = [
        pltpu.roll(rowed[:, t * LANES : (t + 1) * LANES], s, 1) for t in range(BOX // LANES)
    ]
    zero = jnp.zeros((TALL, LANES), jnp.float32)
    for t in range(BOX // LANES + 1):
        left = turned[t - 1] if t > 0 else zero
        here = turned[t] if t < BOX // LANES else zero
        at = pl.ds(pl.multiple_of(j * S + t * LANES, LANES), LANES)
        canvas[:, at] += jnp.where(lane < s, left, here)

    @pl.when(j == per_dev - 1)
    def _():
        n = lax.broadcasted_iota(jnp.int32, (2 * S, S), 0)
        m = lax.broadcasted_iota(jnp.int32, (2 * S, S), 1)
        band = split(blur_weight(n - LANES - m))
        for t in range(wide // S):
            lo, hi = t * S - LANES, t * S + S + LANES
            if lo < 0:
                near = jnp.concatenate([canvas[:, wide + lo :], canvas[:, :hi]], axis=1)
            elif hi > wide:
                near = jnp.concatenate([canvas[:, lo:], canvas[:, : hi - wide]], axis=1)
            else:
                near = canvas[:, lo:hi]
            out = dot_split(split(near), band)
            at = slice(t * S, (t + 1) * S)
            up_ref[:, at] = out[:RADIUS]
            own_ref[:, at] = out[RADIUS : RADIUS + S]
            d1_ref[:, at] = out[RADIUS + S : RADIUS + 2 * S]
            d2_ref[:, at] = out[RADIUS + 2 * S :]


def cell_block():
    return pl.BlockSpec((S, S), lambda j, *_: (0, j))


def box_block():
    return pl.BlockSpec((1, 1, BOX, BOX), lambda j, *_: (0, j, 0, 0))


def moved_by(array, axis, by):
    length = lax.axis_size(axis)
    return lax.ppermute(array, axis, [(i, (i + by) % length) for i in range(length)])


def shifted(field):
    below = moved_by(field[:HALF], "row", -1)
    rowset = jnp.concatenate([field[HALF:], below], axis=0)
    beside = moved_by(rowset[:, :HALF], "col", -1)
    return jnp.concatenate([rowset[:, HALF:], beside], axis=1)


def on_device(source, boxes_a, shifts_a, widths_a, boxes_b, shifts_b, widths_b):
    cols = source.shape[1]
    per_dev = cols // S
    wide = cols + 2 * S
    params = pltpu.CompilerParams(vmem_limit_bytes=56 * 1024 * 1024)

    u_first = pl.pallas_call(
        kernel_a,
        grid_spec=pltpu.PrefetchScalarGridSpec(
            num_scalar_prefetch=2,
            grid=(per_dev,),
            in_specs=[cell_block(), box_block()],
            out_specs=cell_block(),
            scratch_shapes=[pltpu.VMEM((BOX, BOX), jnp.float32)],
        ),
        out_shape=jax.ShapeDtypeStruct((S, cols), jnp.float32),
        compiler_params=params,
        name="aligned",
    )(shifts_a[0], widths_a[0], source, boxes_a)

    whole = lambda h: pl.BlockSpec((h, wide), lambda j, *_: (0, 0))
    up, own, down1, down2 = pl.pallas_call(
        functools.partial(kernel_b, per_dev),
        grid_spec=pltpu.PrefetchScalarGridSpec(
            num_scalar_prefetch=2,
            grid=(per_dev,),
            in_specs=[cell_block(), cell_block(), box_block()],
            out_specs=[whole(h) for h in (RADIUS, S, S, DOWN2)],
            scratch_shapes=[
                pltpu.VMEM((BOX, BOX), jnp.float32),
                pltpu.VMEM((TALL, wide), jnp.float32),
            ],
        ),
        out_shape=[jax.ShapeDtypeStruct((h, wide), jnp.float32) for h in (RADIUS, S, S, DOWN2)],
        compiler_params=params,
        name="shifted",
    )(shifts_b[0], widths_b[0], shifted(source), shifted(u_first), boxes_b)

    total = own + moved_by(down1, "row", 1)
    total = total.at[:DOWN2].add(moved_by(down2, "row", 2))
    total = total.at[S - RADIUS :].add(moved_by(up, "row", -1))
    spill = total[:, cols:]
    x = lax.broadcasted_iota(jnp.int32, (1, 2 * S), 1)
    ahead = moved_by(spill, "col", 1)
    behind = ahead if lax.axis_size("col") == 2 else moved_by(spill[:, -LANES:], "col", -1)
    ahead = jnp.where(x < 2 * S - RADIUS, ahead, 0.0)
    behind = jnp.where(x[:, -LANES:] >= 2 * S - RADIUS, behind[:, -LANES:], 0.0)
    out = total[:, :cols].at[:, : 2 * S].add(ahead)
    return out.at[:, cols - LANES :].add(behind)


def solution(mesh):
    return jax.shard_map(
        on_device,
        mesh=mesh,
        in_specs=(
            P("row", "col"),
            P("row", "col", None, None),
            P("row", "col", None),
            P("row", "col", None),
            P("row", "col", None, None),
            P("row", "col", None),
            P("row", "col", None),
        ),
        out_specs=P("row", "col"),
        check_vma=False,
    )
```

time: 231 us -> 121 us (0.52)
  matrix products: 53.4 us -> 0 us
  Pallas kernels: 0 us -> 40.7 us
  local copies, waits for them, and re-layouts: 43.5 us -> 6.57 us
  waiting for transfers between devices: 86.6 us -> 52 us
  other arithmetic: 27.5 us -> 7.24 us
  loops' own time: 8.16 us -> 0 us
  starting transfers between devices: 10.3 us -> 13.8 us
    dot_general x16 -> x0, matrix products: 53.4 us -> none  [the longest x5 25 us: apply_fwd(): jnp.dot(horizontal_kernel_grid, multiplier_array.astype(jnp.bfloat16), pr...]
    pallas_call x0 -> x2, Pallas kernels: none -> 40.7 us  [the longest x1 27.6 us: on_device(): pl.pallas_call(functools.partial(kernel_b, per_dev), grid_spec=pltpu.Pref...]
    ppermute x9 -> x8, waiting for transfers between devices: 86.6 us -> 52 us  [moved_by(): lax.ppermute(array, axis, [(i, (i + by) % length) for i in range(length)])]
    dynamic_update_slice x4 -> x0, local copies, waits for them, and re-layouts: 30.4 us -> none  [place(): return lax.dynamic_update_slice(canvas, region + plans[index], (top, left))]
    add x9 -> x1, other arithmetic: 19 us -> 1.65 us  [on_device(): total = own + moved_by(down1, 'row', 1)]
    another operation x1 -> x0, loops' own time: 8.16 us -> none  [on_device(): canvas = lax.fori_loop(0, per_dev, place, canvas)]
    squeeze x0 -> x4, local copies, waits for them, and re-layouts: none -> 3.96 us  [the longest x1 1.32 us: on_device(): shifts_a[0]]
    ppermute x9 -> x8, starting transfers between devices: 10.3 us -> 13.8 us  [moved_by(): lax.ppermute(array, axis, [(i, (i + by) % length) for i in range(length)])]
  transfers between devices with their start and end apart: 9 -> 8, of which waited for: 9 -> 6; matrix products, arithmetic and copies ran while one was open for 1% -> 4% of each run, Pallas kernels for 0% -> 0%
where the time goes in v1:
time: 121 us; the launch traced here: 120 us
  waiting for transfers between devices  52 us (43%)
  Pallas kernels  40.7 us (34%)
  starting transfers between devices  13.8 us (11%)
  other arithmetic  7.24 us (6%)
  local copies, waits for them, and re-layouts  6.57 us (5%)
    ppermute x8, waiting for transfers between devices, moved_by(): lax.ppermute(array, axis, [(i, (i + by) % length) for i in range(length)])  52 us
    pallas_call x1, Pallas kernels, on_device(): pl.pallas_call(functools.partial(kernel_b, per_dev), grid_spec=pltpu.Pref...  27.6 us
    ppermute x8, starting transfers between devices, moved_by(): lax.ppermute(array, axis, [(i, (i + by) % length) for i in range(length)])  13.8 us
    pallas_call x1, Pallas kernels, on_device(): pl.pallas_call(kernel_a, grid_spec=pltpu.PrefetchScalarGridSpec(num_scala...  13.2 us
  transfers between devices with their start and end apart: 8, of which 6 were waited for; matrix products, arithmetic and copies ran while one was open for 4% of the time, Pallas kernels for 0%

profile of v1, /device:TPU:1, one launch (start us, length us, event | category | flops | bytes accessed | tf_op | source)
XLA Modules:
  0.0 120.4 jit_solution(268804134354218037)
XLA Ops:
  0.0 1.3 %copy.8.shift_ref = s32[4,2]{1,0:T(4,128)} copy(s32[4,2]{0,1:T(2,128)} %bitcast.6) | data formatting | bytes 64 | tf_op jit(solution)/shard_map/squeeze | solution.py:182
  1.3 1.3 %copy.9.width_ref = s32[4,2]{1,0:T(4,128)} copy(s32[4,2]{0,1:T(2,128)} %bitcast.7) | data formatting | bytes 64 | tf_op jit(solution)/shard_map/squeeze | solution.py:182
  2.6 13.2 %aligned.1 = f32[256,1024]{1,0:T(8,128)} custom-call(s32[4,2]{1,0:T(4,128)} %copy.8.shift_ref, s32[4,2]{1,0:T(4,128)} %copy.9.width_ref, f32[256,1024]{1,0:T(8,128)} %a_ref.1, f32[1,4,512,512]{3,2,1,0:T(8,128)} %box_ref.2), custom_call_target="tpu_custom_call" | custom-call | tf_op jit(solution)/shard_map/aligned/pallas_call | solution.py:170
  15.8 0.0 copy-start
  15.8 1.4 %fusion.7 = (f32[128,1024]{1,0:T(8,128)S(1)}, f32[128,1024]{1,0:T(8,128)S(1)}) fusion(f32[256,1024]{1,0:T(8,128)} %aligned.1), kind=kLoop, calls=%fused_computation.22 | loop fusion | bytes 2097152 | tf_op jit(solution)/shard_map/slice | solution.py:159
  17.2 0.0 copy-start.2
  17.2 0.0 copy-start.3
  17.2 0.1 collective-permute-start.2
  17.3 0.1 copy-done
  17.4 0.1 fusion.8
  17.4 5.4 %collective-permute-start = (f32[128,1024]{1,0:T(8,128)S(1)}, f32[128,1024]{1,0:T(8,128)S(1)}, u32[]{:S(2)}, u32[]{:S(2)}) collective-permute-start(f32[128,1024]{1,0:T(8,128)S(1)} %get-tuple-element.64), channel_id=1, source_target_pairs={{0,30},{2,0},{4,2},{6,4},{8,6},{10,8},{12,10},{14,12},{16,14},{18,... | collective-permute-start | bytes 1572872 | tf_op jit(solution)/shard_map/ppermute | solution.py:154
  22.9 0.0 copy-done.2
  22.9 0.7 copy.10.shift_ref
  23.6 0.0 copy-done.3
  23.6 0.6 copy.11.width_ref
  24.2 2.5 %collective-permute-done.2 = f32[128,1024]{1,0:T(8,128)S(1)} collective-permute-done((f32[128,1024]{1,0:T(8,128)S(1)}, f32[128,1024]{1,0:T(8,128)S(1)}, u32[]{:S(2)}, u32[]{:S(2)}) %collective-permute-start.2) | collective-permute-done | bytes 524320 | tf_op jit(solution)/shard_map/ppermute | solution.py:154
  26.8 1.3 %collective-permute-start.3 = (f32[256,128]{1,0:T(8,128)S(1)}, f32[256,128]{1,0:T(8,128)S(1)}, u32[]{:S(2)}, u32[]{:S(2)}) collective-permute-start(f32[256,128]{1,0:T(8,128)S(1)} %pad_maximum_fusion.2), channel_id=1, source_target_pairs={{0,1},{1,0},{2,3},{3,2},{4,5},{5,4},{6,7},{7,6},{8,9},{9,8},{10,11... | collective-permute-start | bytes 393224 | tf_op jit(solution)/shard_map/ppermute | solution.py:154
  28.0 4.3 %collective-permute-done = f32[128,1024]{1,0:T(8,128)S(1)} collective-permute-done((f32[128,1024]{1,0:T(8,128)S(1)}, f32[128,1024]{1,0:T(8,128)S(1)}, u32[]{:S(2)}, u32[]{:S(2)}) %collective-permute-start) | collective-permute-done | bytes 524320 | tf_op jit(solution)/shard_map/ppermute | solution.py:154
  32.4 1.3 %collective-permute-start.1 = (f32[256,128]{1,0:T(8,128)S(1)}, f32[256,128]{1,0:T(8,128)S(1)}, u32[]{:S(2)}, u32[]{:S(2)}) collective-permute-start(f32[256,128]{1,0:T(8,128)S(1)} %pad_maximum_fusion.3), channel_id=1, source_target_pairs={{0,1},{1,0},{2,3},{3,2},{4,5},{5,4},{6,7},{7,6},{8,9},{9,8},{10,11... | collective-permute-start | bytes 393224 | tf_op jit(solution)/shard_map/ppermute | solution.py:154
  33.7 0.1 fusion
  33.7 0.1 fusion.1
  33.8 0.0 collective-permute-done.3
  33.8 1.1 pad_maximum_fusion.1.u_ref
  34.9 1.3 %collective-permute-done.1 = f32[256,128]{1,0:T(8,128)S(1)} collective-permute-done((f32[256,128]{1,0:T(8,128)S(1)}, f32[256,128]{1,0:T(8,128)S(1)}, u32[]{:S(2)}, u32[]{:S(2)}) %collective-permute-start.1) | collective-permute-done | bytes 131104 | tf_op jit(solution)/shard_map/ppermute | solution.py:154
  36.3 1.1 pad_maximum_fusion.a_ref
  37.4 27.6 %shifted.1 = (f32[8,1536]{1,0:T(8,128)}, f32[256,1536]{1,0:T(8,128)}, f32[256,1536]{1,0:T(8,128)}, f32[136,1536]{1,0:T(8,128)}) custom-call(s32[4,2]{1,0:T(4,128)} %copy.10.shift_ref, s32[4,2]{1,0:T(4,128)} %copy.11.width_ref, f32[256,1024]{1,0:T(8,128)} %pad_maximum_fusion.a_ref, f32[256,1024]{1,0:T(8,128)} %pad_maximum_fusion.1.u_ref, ...), custom_call_target="tpu_custom_call" | custom-call | tf_op jit(solution)/shard_map/shifted/pallas_call | solution.py:185
  64.9 1.0 collective-permute-start.4
  65.9 3.5 %collective-permute-start.5 = (f32[136,1536]{1,0:T(8,128)}, f32[136,1536]{1,0:T(8,128)S(1)}, u32[]{:S(2)}, u32[]{:S(2)}) collective-permute-start(f32[136,1536]{1,0:T(8,128)} %get-tuple-element.59), channel_id=1, source_target_pairs={{0,4},{2,6},{4,8},{6,10},{8,12},{10,14},{12,16},{14,18},{16,20},{1... | collective-permute-start | bytes 2506760 | tf_op jit(solution)/shard_map/ppermute | solution.py:154
  69.4 0.0 collective-permute-start.6
  69.4 23.7 %collective-permute-done.4 = f32[256,1536]{1,0:T(8,128)S(1)} collective-permute-done((f32[256,1536]{1,0:T(8,128)}, f32[256,1536]{1,0:T(8,128)S(1)}, u32[]{:S(2)}, u32[]{:S(2)}) %collective-permute-start.4) | collective-permute-done | bytes 1572896 | tf_op jit(solution)/shard_map/ppermute | solution.py:154
  93.1 1.7 %add.31 = f32[256,1536]{1,0:T(8,128)S(1)} add(f32[256,1536]{1,0:T(8,128)} %get-tuple-element.57, f32[256,1536]{1,0:T(8,128)S(1)} %collective-permute-done.4) | non-fusion elementwise | flops 393216 | bytes 4718592 | tf_op jit(solution)/shard_map/add | solution.py:202
  94.7 14.0 %collective-permute-done.5 = f32[136,1536]{1,0:T(8,128)S(1)} collective-permute-done((f32[136,1536]{1,0:T(8,128)}, f32[136,1536]{1,0:T(8,128)S(1)}, u32[]{:S(2)}, u32[]{:S(2)}) %collective-permute-start.5) | collective-permute-done | bytes 835616 | tf_op jit(solution)/shard_map/ppermute | solution.py:154
  108.7 0.2 fusion.2
  109.0 0.0 collective-permute-done.6
  109.0 1.3 %collective-permute-start.7 = (f32[256,512]{1,0:T(8,128)S(1)}, f32[256,512]{1,0:T(8,128)S(1)}, u32[]{:S(2)}, u32[]{:S(2)}) collective-permute-start(f32[256,512]{1,0:T(8,128)S(1)} %slice.139), channel_id=1, source_target_pairs={{0,1},{1,0},{2,3},{3,2},{4,5},{5,4},{6,7},{7,6},{8,9},{9,8},{10,11... | collective-permute-start | bytes 1572872 | tf_op jit(solution)/shard_map/ppermute | solution.py:154
  110.3 0.6 compare_reduce_fusion
  111.0 0.1 slice.137
  111.0 6.1 %collective-permute-done.7 = f32[256,512]{1,0:T(8,128)S(1)} collective-permute-done((f32[256,512]{1,0:T(8,128)S(1)}, f32[256,512]{1,0:T(8,128)S(1)}, u32[]{:S(2)}, u32[]{:S(2)}) %collective-permute-start.7) | collective-permute-done | bytes 524320 | tf_op jit(solution)/shard_map/ppermute | solution.py:154
  117.1 0.8 fusion.3
  117.9 0.0 copy-start.1
  117.9 1.0 copy-done.1
  118.9 1.6 %fusion.5 = f32[256,1024]{1,0:T(8,128)} fusion(f32[256,1024]{1,0:T(8,128)} %copy-done.1, f32[256,512]{1,0:T(8,128)S(1)} %collective-permute-done.7, pred[128]{0:T(512)(128)(4,1)S(1)} %compare_bitcast_fusion), kind=kLoop, calls=%fused_computation.14 | loop fusion | flops 65536 | bytes 393344 | tf_op jit(solution)/shard_map/scatter-add | solution.py:212
  (6 shorter events, 0.1 us)
Async XLA Ops:
  15.8 1.5 %copy-start = (f32[256,1024]{1,0:T(8,128)S(1)}, f32[256,1024]{1,0:T(8,128)}, u32[]{:S(2)}) copy-start(f32[256,1024]{1,0:T(8,128)} %a_ref.1) | copy-start | bytes 3145732
  17.2 5.7 %copy-start.2 = (s32[1,4,2]{1,2,0:T(2,128)S(1)}, s32[1,4,2]{1,2,0:T(2,128)}, u32[]{:S(2)}) copy-start(s32[1,4,2]{1,2,0:T(2,128)} %param.20) | copy-start | bytes 100
  17.2 6.4 %copy-start.3 = (s32[1,4,2]{1,2,0:T(2,128)S(1)}, s32[1,4,2]{1,2,0:T(2,128)}, u32[]{:S(2)}) copy-start(s32[1,4,2]{1,2,0:T(2,128)} %param.21) | copy-start | bytes 100
  17.2 9.5 %collective-permute-start.2 = (f32[128,1024]{1,0:T(8,128)S(1)}, f32[128,1024]{1,0:T(8,128)S(1)}, u32[]{:S(2)}, u32[]{:S(2)}) collective-permute-start(f32[128,1024]{1,0:T(8,128)S(1)} %get-tuple-element.62), channel_id=1, source_target_pairs={{0,30},{2,0},{4,2},{6,4},{8,6},{10,8},{12,10},{14,12},{16,14},{18,... | collective-permute-start | bytes 1572872 | tf_op jit(solution)/shard_map/ppermute | solution.py:154
  17.4 14.9 %collective-permute-start = (f32[128,1024]{1,0:T(8,128)S(1)}, f32[128,1024]{1,0:T(8,128)S(1)}, u32[]{:S(2)}, u32[]{:S(2)}) collective-permute-start(f32[128,1024]{1,0:T(8,128)S(1)} %get-tuple-element.64), channel_id=1, source_target_pairs={{0,30},{2,0},{4,2},{6,4},{8,6},{10,8},{12,10},{14,12},{16,14},{18,... | collective-permute-start | bytes 1572872 | tf_op jit(solution)/shard_map/ppermute | solution.py:154
  26.8 7.1 %collective-permute-start.3 = (f32[256,128]{1,0:T(8,128)S(1)}, f32[256,128]{1,0:T(8,128)S(1)}, u32[]{:S(2)}, u32[]{:S(2)}) collective-permute-start(f32[256,128]{1,0:T(8,128)S(1)} %pad_maximum_fusion.2), channel_id=1, source_target_pairs={{0,1},{1,0},{2,3},{3,2},{4,5},{5,4},{6,7},{7,6},{8,9},{9,8},{10,11... | collective-permute-start | bytes 393224 | tf_op jit(solution)/shard_map/ppermute | solution.py:154
  32.4 3.9 %collective-permute-start.1 = (f32[256,128]{1,0:T(8,128)S(1)}, f32[256,128]{1,0:T(8,128)S(1)}, u32[]{:S(2)}, u32[]{:S(2)}) collective-permute-start(f32[256,128]{1,0:T(8,128)S(1)} %pad_maximum_fusion.3), channel_id=1, source_target_pairs={{0,1},{1,0},{2,3},{3,2},{4,5},{5,4},{6,7},{7,6},{8,9},{9,8},{10,11... | collective-permute-start | bytes 393224 | tf_op jit(solution)/shard_map/ppermute | solution.py:154
  64.9 28.1 %collective-permute-start.4 = (f32[256,1536]{1,0:T(8,128)}, f32[256,1536]{1,0:T(8,128)S(1)}, u32[]{:S(2)}, u32[]{:S(2)}) collective-permute-start(f32[256,1536]{1,0:T(8,128)} %get-tuple-element.58), channel_id=1, source_target_pairs={{0,2},{2,4},{4,6},{6,8},{8,10},{10,12},{12,14},{14,16},{16,18},{18... | collective-permute-start | bytes 4718600 | tf_op jit(solution)/shard_map/ppermute | solution.py:154
  65.9 42.8 %collective-permute-start.5 = (f32[136,1536]{1,0:T(8,128)}, f32[136,1536]{1,0:T(8,128)S(1)}, u32[]{:S(2)}, u32[]{:S(2)}) collective-permute-start(f32[136,1536]{1,0:T(8,128)} %get-tuple-element.59), channel_id=1, source_target_pairs={{0,4},{2,6},{4,8},{6,10},{8,12},{10,14},{12,16},{14,18},{16,20},{1... | collective-permute-start | bytes 2506760 | tf_op jit(solution)/shard_map/ppermute | solution.py:154
  69.4 39.6 %collective-permute-start.6 = (f32[8,1536]{1,0:T(8,128)}, f32[8,1536]{1,0:T(8,128)S(1)}, u32[]{:S(2)}, u32[]{:S(2)}) collective-permute-start(f32[8,1536]{1,0:T(8,128)} %get-tuple-element.60), channel_id=1, source_target_pairs={{0,30},{2,0},{4,2},{6,4},{8,6},{10,8},{12,10},{14,12},{16,14},{18,... | collective-permute-start | bytes 147464 | tf_op jit(solution)/shard_map/ppermute | solution.py:154
  109.0 8.1 %collective-permute-start.7 = (f32[256,512]{1,0:T(8,128)S(1)}, f32[256,512]{1,0:T(8,128)S(1)}, u32[]{:S(2)}, u32[]{:S(2)}) collective-permute-start(f32[256,512]{1,0:T(8,128)S(1)} %slice.139), channel_id=1, source_target_pairs={{0,1},{1,0},{2,3},{3,2},{4,5},{5,4},{6,7},{7,6},{8,9},{9,8},{10,11... | collective-permute-start | bytes 1572872 | tf_op jit(solution)/shard_map/ppermute | solution.py:154
  117.9 1.0 copy-start.1

commit v2 on v1

v2 whole, which is shorter than its diff:
```python
import functools
import math

import jax
import jax.numpy as jnp
from jax import lax
from jax.experimental import pallas as pl
from jax.experimental.pallas import tpu as pltpu
from jax.sharding import PartitionSpec as P

S = 256
BOX = 512
ITERS = 3
RADIUS = 8
LANES = 128
HALF = S // 2
DOWN2 = HALF + RADIUS
TALL = RADIUS + 2 * S + DOWN2

kernel_eps = 0.05
blur_sigma = 2.0
blur_total = sum(
    math.exp(-(d * d) / (2.0 * blur_sigma * blur_sigma)) for d in range(-RADIUS, RADIUS + 1)
)


def gauss(offset, shape, box_dim):
    k = lax.broadcasted_iota(jnp.int32, shape, box_dim)
    p = lax.broadcasted_iota(jnp.int32, shape, 1 - box_dim)
    dist = (offset + k - p).astype(jnp.float32) * (1.0 / S)
    return jnp.exp(dist * dist * (-1.0 / kernel_eps)).astype(jnp.bfloat16)


def blur_weight(d):
    f = d.astype(jnp.float32)
    w = jnp.exp(f * f * (-1.0 / (2.0 * blur_sigma * blur_sigma))) * (1.0 / blur_total)
    return jnp.where(jnp.abs(d) <= RADIUS, w, 0.0)


def split(x):
    hi = x.astype(jnp.bfloat16)
    return hi, (x - hi.astype(jnp.float32)).astype(jnp.bfloat16)


def dot(a, b):
    return jnp.dot(a, b, preferred_element_type=jnp.float32)


def dot_t(a, b):
    return lax.dot_general(a, b, (((1,), (1,)), ((), ())), preferred_element_type=jnp.float32)


def dot_split(a, b):
    (ah, al), (bh, bl) = a, b
    return dot(ah, bh) + (dot(ah, bl) + dot(al, bh))


def bf(x):
    return x.astype(jnp.bfloat16)


def target_of(box_ref, height, width):
    rows = lax.broadcasted_iota(jnp.int32, (BOX, BOX), 0)
    cols = lax.broadcasted_iota(jnp.int32, (BOX, BOX), 1)
    return jnp.where((rows < height) & (cols < width), box_ref[0, 0], 0.0)


MESH = pl.DeviceIdType.MESH
OWN = slice(RADIUS, RADIUS + S)


def tiles(first, count):
    return slice(first * LANES, (first + count) * LANES)


def units_of(per_dev):
    units = [(per_dev - 2, 2 * per_dev, 3)]
    units += [(j, 2 * j + 4, 2) for j in range(per_dev - 3, 0, -1)]
    units += [(0, 2 * per_dev + 3, 1), (0, 0, 3), (0, 3, 3)]
    return units


def kernel(
    per_dev,
    n_row,
    n_col,
    info,
    src,
    box_a,
    box_b,
    out,
    tgt,
    u_loc,
    mv_s,
    mv_u,
    canvas,
    bl,
    r1,
    r2,
    rup,
    cs,
    cl,
    s_send,
    s_recv,
    u_send,
    u_recv,
    x_send,
    x_recv,
    c_send,
    c_recv,
):
    g = pl.program_id(0)
    cols = per_dev * S
    wide = cols + 2 * S
    row, col = lax.axis_index("row"), lax.axis_index("col")
    odd = lax.rem(row, 2) == 1
    even = lax.rem(row, 2) == 0
    units = units_of(per_dev)

    def at(dr, dc):
        return (lax.rem(row + dr + n_row, n_row), lax.rem(col + dc + n_col, n_col))

    def remote(a, b, send, recv, to):
        return pltpu.make_async_remote_copy(
            src_ref=a, dst_ref=b, send_sem=send, recv_sem=recv, device_id=to, device_id_type=MESH
        )

    upper, lower = slice(0, HALF), slice(HALF, S)
    edge = slice(cols - LANES, cols)

    def halo(field, moved, k, send, recv):
        if k == 0:
            a, b, to = field.at[upper, HALF:], moved.at[lower, : cols - HALF], at(-1, 0)
        elif k == 1:
            a, b, to = field.at[upper, :LANES], moved.at[lower, edge], at(-1, -1)
        else:
            a, b, to = field.at[lower, :LANES], moved.at[upper, edge], at(0, -1)
        return remote(a, b, send.at[k], recv.at[k], to)

    def chunk(j):
        lo, hi = max(j * S, HALF), (j + 1) * S
        return remote(
            u_loc.at[upper, lo:hi],
            mv_u.at[lower, lo - HALF : hi - HALF],
            u_send.at[2 + j],
            u_recv.at[2 + j],
            at(-1, 0),
        )

    def corner(k):
        a = u_loc.at[upper, :LANES] if k == 0 else u_loc.at[lower, :LANES]
        b = mv_u.at[lower, edge] if k == 0 else mv_u.at[upper, edge]
        return remote(a, b, u_send.at[k], u_recv.at[k], at(-1, -1) if k == 0 else at(0, -1))

    def spill(n, kind):
        _, first, count = units[n]
        c = tiles(first, count)
        if kind == 0:
            a, b, to = bl.at[RADIUS + S :, c], r1.at[:, c], at(1, 0)
        elif kind == 1:
            a, b, to = bl.at[RADIUS + S : RADIUS + 2 * S, c], r1.at[:S, c], at(1, 0)
        elif kind == 2:
            a, b, to = bl.at[RADIUS + 2 * S :, c], r2.at[:, c], at(2, 0)
        else:
            a, b, to = bl.at[:RADIUS, c], rup.at[:, c], at(-1, 0)
        k = {0: 0, 1: 0, 2: 1, 3: 2}[kind]
        return remote(a, b, x_send.at[n, k], x_recv.at[n, k], to)

    def beside(k):
        if k == 0:
            a, b, to = bl.at[OWN, cols : cols + 3 * LANES], cs.at[:, : 3 * LANES], at(0, 1)
        elif k == 1:
            a, b, to = bl.at[OWN, cols + 3 * LANES :], cs.at[:, 3 * LANES :], at(0, 1)
        else:
            a, b, to = bl.at[OWN, cols + 3 * LANES :], cl, at(0, -1)
        return remote(a, b, c_send.at[k], c_recv.at[k], to)

    sides = 2 if n_col == 2 else 3

    def hand_on(n):
        @pl.when(odd)
        def _():
            c = tiles(units[n][1], units[n][2])
            spill(n, 0).wait_recv()
            bl[RADIUS + S : RADIUS + S + DOWN2, c] += r1[S:, c]
            spill(n, 1).start()
            spill(n, 2).start()

    def give(n):
        spill(n, 3).start()

        @pl.when(even)
        def _():
            spill(n, 0).start()

    def smooth(first, count, band):
        lo, hi = (first - 1) * LANES, (first + count + 1) * LANES
        if lo < 0:
            near = jnp.concatenate([canvas[:, wide + lo :], canvas[:, :hi]], axis=1)
        elif hi > wide:
            near = jnp.concatenate([canvas[:, lo:], canvas[:, : hi - wide]], axis=1)
        else:
            near = canvas[:, lo:hi]
        res = dot_split(split(near), [b[: (count + 2) * LANES, : count * LANES] for b in band])
        if first * LANES + count * LANES > wide:
            bl[:, first * LANES :] = res[:, :LANES]
            bl[:, :LANES] = res[:, LANES:]
        else:
            bl[:, tiles(first, count)] = res

    def the_band():
        n = lax.broadcasted_iota(jnp.int32, (2 * S, S), 0)
        m = lax.broadcasted_iota(jnp.int32, (2 * S, S), 1)
        return split(blur_weight(n - LANES - m))

    def folded(n, dest):
        c = tiles(units[n][1], units[n][2])

        @pl.when(even)
        def _():
            spill(n, 1).wait_recv()
            dest[...] = bl[OWN, c] + r1[:S, c]

        @pl.when(odd)
        def _():
            spill(n, 2).wait_recv()
            mine = bl[OWN, c] + r1[:S, c]
            dest[...] = mine
            dest[:DOWN2] += r2[:, c]

        spill(n, 3).wait_recv()
        dest[S - RADIUS :] += rup[:, c]

    @pl.when(g < per_dev)
    def _():
        barrier = pltpu.get_barrier_semaphore()
        peers = [(-1, 0), (1, 0), (-2, 0), (2, 0), (0, -1), (0, 1), (-1, -1), (1, 1)]

        @pl.when(g == 0)
        def _():
            for dr, dc in peers:
                pl.semaphore_signal(barrier, inc=1, device_id=at(dr, dc), device_id_type=MESH)
            mv_s[upper, : cols - HALF] = src[lower, HALF:]
            canvas[...] = jnp.zeros_like(canvas)

        j = lax.rem(per_dev - g, per_dev)
        o_r, o_c = info[2 * j], info[2 * j + 1]
        h, w = info[2 * per_dev + 2 * j], info[2 * per_dev + 2 * j + 1]
        kr = gauss(o_r, (S, BOX), 1)
        krt = gauss(o_r, (BOX, S), 0)
        kc = gauss(o_c, (S, BOX), 1)
        tgt[...] = target_of(box_a, h, w)
        here = pl.ds(pl.multiple_of(j * S, S), S)
        a = src[:, here]
        in_r = bf(jnp.sum(krt.astype(jnp.float32), axis=1, keepdims=True)).astype(jnp.float32)
        in_c = jnp.sum(kc.astype(jnp.float32), axis=0, keepdims=True)
        back = in_r * in_c
        for step in range(ITERS):
            v = bf(tgt[...] / back)
            u = a / dot_t(bf(dot(kr, v)), kc)
            if step < ITERS - 1:
                back = dot(bf(dot(krt, bf(u))), kc)
        u_loc[:, here] = u

        @pl.when(g == 0)
        def _():
            pl.semaphore_wait(barrier, len(peers))
            for k in range(3):
                halo(src, mv_s, k, s_send, s_recv).start()
            for k in range(2):
                corner(k).start()

        for i in range(per_dev):

            @pl.when(j == i)
            def _():
                chunk(i).start()
                lo, hi = max(i * S, HALF), (i + 1) * S
                mv_u[upper, lo - HALF : hi - HALF] = u_loc[lower, lo:hi]

    @pl.when(g >= per_dev)
    def _():
        j = 2 * per_dev - 1 - g

        @pl.when(j == per_dev - 1)
        def _():
            for k in range(3):
                halo(src, mv_s, k, s_send, s_recv).wait_recv()
            for k in range(2):
                corner(k).wait_recv()

        for i in range(per_dev):

            @pl.when(j == i)
            def _():
                chunk(i).wait_recv()

        base = 4 * per_dev
        o_r, o_c = info[base + 2 * j], info[base + 2 * j + 1]
        h, w = info[base + 2 * per_dev + 2 * j], info[base + 2 * per_dev + 2 * j + 1]
        kr = gauss(o_r, (S, BOX), 1)
        krt = gauss(o_r, (BOX, S), 0)
        kc = gauss(o_c, (S, BOX), 1)
        tgt[...] = target_of(box_b, h, w)
        here = pl.ds(pl.multiple_of(j * S, S), S)
        a = mv_s[:, here]
        u = mv_u[:, here]
        for step in range(ITERS):
            back = dot(bf(dot(krt, bf(u))), kc)
            v = tgt[...] / back
            u = a / dot_t(bf(dot(kr, bf(v))), kc)
            if step == 0:
                for n, (when, _, _) in enumerate(units):
                    if when > 0:

                        @pl.when(j == when - 1)
                        def _():
                            hand_on(n)

        plan = v * dot(bf(dot(krt, bf(u))), kc)

        y = lax.broadcasted_iota(jnp.int32, (TALL, BOX), 0) - RADIUS
        k = lax.broadcasted_iota(jnp.int32, (TALL, BOX), 1)
        rowed = dot_split(split(blur_weight(HALF + o_r + k - y)), split(plan))
        s = HALF + o_c
        lane = lax.broadcasted_iota(jnp.int32, (TALL, LANES), 1)
        turned = [pltpu.roll(rowed[:, tiles(t, 1)], s, 1) for t in range(BOX // LANES)]
        zero = jnp.zeros((TALL, LANES), jnp.float32)
        for t in range(BOX // LANES + 1):
            left = turned[t - 1] if t > 0 else zero
            right = turned[t] if t < BOX // LANES else zero
            spot = pl.ds(pl.multiple_of(j * S + t * LANES, LANES), LANES)
            canvas[:, spot] += jnp.where(lane < s, left, right)

        for n, (when, first, count) in enumerate(units):
            if when > 0:

                @pl.when(j == when)
                def _():
                    band = the_band()
                    for f in range(first, first + count, 2):
                        smooth(f, min(2, first + count - f), band)
                    give(n)

        @pl.when(j == 0)
        def _():
            band = the_band()
            late = [n for n, u_ in enumerate(units) if u_[0] == 0]
            corner_unit, left_unit, right_unit = late
            smooth(2 * per_dev + 3, 2, band)
            give(corner_unit)
            mid = units[left_unit][2]
            last = units[right_unit][1] + units[right_unit][2]
            for f in range(1, mid, 2):
                smooth(f, min(2, mid - f), band)
            give(left_unit)
            hand_on(corner_unit)
            for f in range(mid, last, 2):
                smooth(f, min(2, last - f), band)
            give(right_unit)
            hand_on(left_unit)
            hand_on(right_unit)

            folded(0, bl.at[OWN, tiles(units[0][1], units[0][2])])
            beside(0).start()
            for n in range(1, len(units) - 3):
                folded(n, out.at[:, tiles(units[n][1], units[n][2])])
            folded(corner_unit, bl.at[OWN, tiles(units[corner_unit][1], units[corner_unit][2])])
            for k in range(1, sides):
                beside(k).start()
            folded(left_unit, out.at[:, tiles(units[left_unit][1], units[left_unit][2])])
            folded(right_unit, out.at[:, tiles(units[right_unit][1], units[right_unit][2])])

            ln = lax.broadcasted_iota(jnp.int32, (S, LANES), 1)
            for k in range(sides):
                beside(k).wait_recv()
            out[:, : 3 * LANES] += cs[:, : 3 * LANES]
            out[:, 3 * LANES : 4 * LANES] += jnp.where(ln < LANES - RADIUS, cs[:, 3 * LANES :], 0.0)
            behind = cs[:, 3 * LANES :] if n_col == 2 else cl[...]
            out[:, edge] += jnp.where(ln >= LANES - RADIUS, behind, 0.0)

            for k in range(3):
                halo(src, mv_s, k, s_send, s_recv).wait_send()
            for k in range(2):
                corner(k).wait_send()
            for i in range(per_dev):
                chunk(i).wait_send()
            for k in range(sides):
                beside(k).wait_send()
            for n in range(len(units)):
                spill(n, 3).wait_send()

                @pl.when(even)
                def _():
                    spill(n, 0).wait_send()

                @pl.when(odd)
                def _():
                    spill(n, 1).wait_send()
                    spill(n, 2).wait_send()


def on_device(n_row, n_col, source, boxes_a, shifts_a, widths_a, boxes_b, shifts_b, widths_b):
    cols = source.shape[1]
    per_dev = cols // S
    wide = cols + 2 * S
    units = len(units_of(per_dev))
    info = jnp.concatenate([shifts_a, widths_a, shifts_b, widths_b]).reshape(-1)
    f32 = lambda *shape: pltpu.VMEM(shape, jnp.float32)
    dma = pltpu.SemaphoreType.DMA
    box = (1, 1, BOX, BOX)
    first = lambda g, *_: (0, lax.rem(per_dev - jnp.minimum(g, per_dev - 1), per_dev), 0, 0)
    second = lambda g, *_: (0, jnp.minimum(2 * per_dev - 1 - g, per_dev - 1), 0, 0)
    return pl.pallas_call(
        functools.partial(kernel, per_dev, n_row, n_col),
        grid_spec=pltpu.PrefetchScalarGridSpec(
            num_scalar_prefetch=1,
            grid=(2 * per_dev,),
            in_specs=[
                pl.BlockSpec((S, cols), lambda g, *_: (0, 0)),
                pl.BlockSpec(box, first),
                pl.BlockSpec(box, second),
            ],
            out_specs=pl.BlockSpec((S, cols), lambda g, *_: (0, 0)),
            scratch_shapes=[
                f32(BOX, BOX),
                f32(S, cols),
                f32(S, cols),
                f32(S, cols),
                f32(TALL, wide),
                f32(TALL, wide),
                f32(S + DOWN2, wide),
                f32(DOWN2, wide),
                f32(RADIUS, wide),
                f32(S, 2 * S),
                f32(S, LANES),
                dma((3,)),
                dma((3,)),
                dma((2 + per_dev,)),
                dma((2 + per_dev,)),
                dma((units, 3)),
                dma((units, 3)),
                dma((3,)),
                dma((3,)),
            ],
        ),
        out_shape=jax.ShapeDtypeStruct((S, cols), jnp.float32),
        compiler_params=pltpu.CompilerParams(
            vmem_limit_bytes=56 * 1024 * 1024, collective_id=0, has_side_effects=True
        ),
        name="transport",
    )(info, source, boxes_a, boxes_b)


def solution(mesh):
    return jax.shard_map(
        functools.partial(on_device, mesh.shape["row"], mesh.shape["col"]),
        mesh=mesh,
        in_specs=(
            P("row", "col"),
            P("row", "col", None, None),
            P("row", "col", None),
            P("row", "col", None),
            P("row", "col", None, None),
            P("row", "col", None),
            P("row", "col", None),
        ),
        out_specs=P("row", "col"),
        check_vma=False,
    )
```

time: 121 us -> 69.7 us (0.58)
  waiting for transfers between devices: 52 us -> 0 us
  Pallas kernels: 40.7 us -> 65.7 us
  starting transfers between devices: 13.8 us -> 0 us
  other arithmetic: 7.24 us -> 0.73 us
  local copies, waits for them, and re-layouts: 6.57 us -> 3.03 us
    ppermute x8 -> x0, waiting for transfers between devices: 52 us -> none  [moved_by(): lax.ppermute(array, axis, [(i, (i + by) % length) for i in range(length)])]
    pallas_call x2 -> x1, Pallas kernels: 40.7 us -> 65.7 us  [on_device(): pl.pallas_call(functools.partial(kernel, per_dev, n_row, n_col), grid_spe...]
    ppermute x8 -> x0, starting transfers between devices: 13.8 us -> none  [moved_by(): lax.ppermute(array, axis, [(i, (i + by) % length) for i in range(length)])]
    squeeze x4 -> x0, local copies, waits for them, and re-layouts: 3.96 us -> none  [the longest x1 1.32 us: on_device(): shifts_a[0]]
    scatter-add x4 -> x0, other arithmetic: 2.55 us -> none  [the longest x1 1.58 us: on_device(): return out.at[:, cols - LANES:].add(behind)]
    add x1 -> x0, other arithmetic: 1.65 us -> none  [on_device(): total = own + moved_by(down1, 'row', 1)]
    concatenate x6 -> x1, other arithmetic: 2.38 us -> 0.73 us  [on_device(): info = jnp.concatenate([shifts_a, widths_a, shifts_b, widths_b]).reshape(-1)]
    slice x4 -> x0, local copies, waits for them, and re-layouts: 1.54 us -> none  [the longest x2 1.43 us: shifted(): rowset = jnp.concatenate([field[HALF:], below], axis=0)]
  transfers between devices with their start and end apart: 8 -> 0, of which waited for: 6 -> 0; matrix products, arithmetic and copies ran while one was open for 4% -> 0% of each run, Pallas kernels for 0% -> 0%
where the time goes in v2:
time: 69.7 us; the launch traced here: 69.5 us
  Pallas kernels  65.7 us (94%)
  local copies, waits for them, and re-layouts  3.03 us (4%)
  other arithmetic  0.73 us (1%)
    pallas_call x1, Pallas kernels, on_device(): pl.pallas_call(functools.partial(kernel, per_dev, n_row, n_col), grid_spe...  65.7 us
    unnamed x1, local copies, waits for them, and re-layouts  2.31 us

profile of v2, /device:TPU:1, one launch (start us, length us, event | category | flops | bytes accessed | tf_op | source)
XLA Modules:
  0.0 69.5 jit_solution(1724857701924675944)
XLA Ops:
  0.0 0.7 %pad_add_fusion = s32[4,4,2]{1,2,0:T(2,128)S(1)} fusion(s32[1,4,2]{1,2,0:T(2,128)} %param.13, s32[1,4,2]{1,2,0:T(2,128)} %param.12, s32[1,4,2]{1,2,0:T(2,128)} %param.10, s32[1,4,2]{1,2,0:T(2,128)} %param.9), kind=kLoop, calls=%fused_computation | loop fusion | flops 96 | bytes 256 | tf_op jit(solution)/shard_map/concatenate | solution.py:408
  0.7 0.1 copy.9
  0.8 0.6 reshape.3.info
  1.5 65.7 %transport.1 = f32[256,1024]{1,0:T(8,128)} custom-call(s32[32]{0:T(128)} %reshape.3.info, f32[256,1024]{1,0:T(8,128)} %src.1, f32[1,4,512,512]{3,2,1,0:T(8,128)} %box_a.1, f32[1,4,512,512]{3,2,1,0:T(8,128)} %box_b.1), custom_call_target="tpu_custom_call" | custom-call | tf_op jit(solution)/shard_map/transport/pallas_call | solution.py:414
  67.2 2.3 %copy.11 = f32[256,1024]{1,0:T(8,128)} copy(f32[256,1024]{1,0:T(8,128)} %transport.1) | data formatting | bytes 2097152

commit v3 on v2

--- a/solution.py
+++ b/solution.py
@@ -24,10 +24,22 @@
 )
 
 
-def gauss(offset, shape, box_dim):
-    k = lax.broadcasted_iota(jnp.int32, shape, box_dim)
-    p = lax.broadcasted_iota(jnp.int32, shape, 1 - box_dim)
-    dist = (offset + k - p).astype(jnp.float32) * (1.0 / S)
+def gauss(offset):
+    shape = (LANES, BOX + LANES)
+    d = lax.broadcasted_iota(jnp.int32, shape, 1) - lax.broadcasted_iota(jnp.int32, shape, 0)
+    g = gauss_of(offset - LANES + d)
+    return jnp.concatenate([g[:, LANES:], g[:, :BOX]], axis=0)
+
+
+def gauss_t(offset):
+    shape = (BOX + LANES, LANES)
+    d = lax.broadcasted_iota(jnp.int32, shape, 0) - lax.broadcasted_iota(jnp.int32, shape, 1)
+    g = gauss_of(offset - LANES + d)
+    return jnp.concatenate([g[LANES:], g[:BOX]], axis=1)
+
+
+def gauss_of(d):
+    dist = d.astype(jnp.float32) * (1.0 / S)
     return jnp.exp(dist * dist * (-1.0 / kernel_eps)).astype(jnp.bfloat16)
 
 
@@ -95,6 +107,8 @@
     mv_u,
     canvas,
     bl,
+    band_hi,
+    band_lo,
     r1,
     r2,
     rup,
@@ -193,7 +207,7 @@
         def _():
             spill(n, 0).start()
 
-    def smooth(first, count, band):
+    def smooth(first, count):
         lo, hi = (first - 1) * LANES, (first + count + 1) * LANES
         if lo < 0:
             near = jnp.concatenate([canvas[:, wide + lo :], canvas[:, :hi]], axis=1)
@@ -201,7 +215,7 @@
             near = jnp.concatenate([canvas[:, lo:], canvas[:, : hi - wide]], axis=1)
         else:
             near = canvas[:, lo:hi]
-        res = dot_split(split(near), [b[: (count + 2) * LANES, : count * LANES] for b in band])
+        res = dot_split(split(near), [b[: (count + 2) * LANES, : count * LANES] for b in (band_hi, band_lo)])
         if first * LANES + count * LANES > wide:
             bl[:, first * LANES :] = res[:, :LANES]
             bl[:, :LANES] = res[:, LANES:]
@@ -242,13 +256,14 @@
                 pl.semaphore_signal(barrier, inc=1, device_id=at(dr, dc), device_id_type=MESH)
             mv_s[upper, : cols - HALF] = src[lower, HALF:]
             canvas[...] = jnp.zeros_like(canvas)
+            band_hi[...], band_lo[...] = the_band()
 
         j = lax.rem(per_dev - g, per_dev)
         o_r, o_c = info[2 * j], info[2 * j + 1]
         h, w = info[2 * per_dev + 2 * j], info[2 * per_dev + 2 * j + 1]
-        kr = gauss(o_r, (S, BOX), 1)
-        krt = gauss(o_r, (BOX, S), 0)
-        kc = gauss(o_c, (S, BOX), 1)
+        kr = gauss(o_r)
+        krt = gauss_t(o_r)
+        kc = gauss(o_c)
         tgt[...] = target_of(box_a, h, w)
         here = pl.ds(pl.multiple_of(j * S, S), S)
         a = src[:, here]
@@ -298,9 +313,9 @@
         base = 4 * per_dev
         o_r, o_c = info[base + 2 * j], info[base + 2 * j + 1]
         h, w = info[base + 2 * per_dev + 2 * j], info[base + 2 * per_dev + 2 * j + 1]
-        kr = gauss(o_r, (S, BOX), 1)
-        krt = gauss(o_r, (BOX, S), 0)
-        kc = gauss(o_c, (S, BOX), 1)
+        kr = gauss(o_r)
+        krt = gauss_t(o_r)
+        kc = gauss(o_c)
         tgt[...] = target_of(box_b, h, w)
         here = pl.ds(pl.multiple_of(j * S, S), S)
         a = mv_s[:, here]
@@ -319,9 +334,22 @@
 
         plan = v * dot(bf(dot(krt, bf(u))), kc)
 
-        y = lax.broadcasted_iota(jnp.int32, (TALL, BOX), 0) - RADIUS
-        k = lax.broadcasted_iota(jnp.int32, (TALL, BOX), 1)
-        rowed = dot_split(split(blur_weight(HALF + o_r + k - y)), split(plan))
+        r = lax.broadcasted_iota(jnp.int32, (LANES, 3 * LANES), 0) - RADIUS
+        m = lax.broadcasted_iota(jnp.int32, (LANES, 3 * LANES), 1) - 2 * LANES
+        weights = split(blur_weight(HALF + o_r + m - r))
+        halves = split(plan)
+        parts = []
+        for b in range(-(-TALL // LANES)):
+            height = min(LANES, TALL - b * LANES)
+            lo, hi = max(b - 2, 0), min(b + 1, BOX // LANES)
+            wt = slice((lo - b + 2) * LANES, (hi - b + 2) * LANES)
+            parts.append(
+                dot_split(
+                    [x[:height, wt] for x in weights],
+                    [x[lo * LANES : hi * LANES] for x in halves],
+                )
+            )
+        rowed = jnp.concatenate(parts, axis=0)
         s = HALF + o_c
         lane = lax.broadcasted_iota(jnp.int32, (TALL, LANES), 1)
         turned = [pltpu.roll(rowed[:, tiles(t, 1)], s, 1) for t in range(BOX // LANES)]
@@ -337,26 +365,24 @@
 
                 @pl.when(j == when)
                 def _():
-                    band = the_band()
                     for f in range(first, first + count, 2):
-                        smooth(f, min(2, first + count - f), band)
+                        smooth(f, min(2, first + count - f))
                     give(n)
 
         @pl.when(j == 0)
         def _():
-            band = the_band()
             late = [n for n, u_ in enumerate(units) if u_[0] == 0]
             corner_unit, left_unit, right_unit = late
-            smooth(2 * per_dev + 3, 2, band)
+            smooth(2 * per_dev + 3, 2)
             give(corner_unit)
             mid = units[left_unit][2]
             last = units[right_unit][1] + units[right_unit][2]
             for f in range(1, mid, 2):
-                smooth(f, min(2, mid - f), band)
+                smooth(f, min(2, mid - f))
             give(left_unit)
             hand_on(corner_unit)
             for f in range(mid, last, 2):
-                smooth(f, min(2, last - f), band)
+                smooth(f, min(2, last - f))
             give(right_unit)
             hand_on(left_unit)
             hand_on(right_unit)
@@ -429,6 +455,8 @@
                 f32(S, cols),
                 f32(TALL, wide),
                 f32(TALL, wide),
+                pltpu.VMEM((2 * S, S), jnp.bfloat16),
+                pltpu.VMEM((2 * S, S), jnp.bfloat16),
                 f32(S + DOWN2, wide),
                 f32(DOWN2, wide),
                 f32(RADIUS, wide),

time: 69.7 us -> 66.4 us (0.953)
  Pallas kernels: 65.7 us -> 62.4 us
    pallas_call x1, Pallas kernels: 65.7 us -> 62.4 us  [on_device(): pl.pallas_call(functools.partial(kernel, per_dev, n_row, n_col), grid_spe...]
where the time goes in v3:
time: 66.4 us; the launch traced here: 66.2 us
  Pallas kernels  62.4 us (94%)
  local copies, waits for them, and re-layouts  3.03 us (5%)
  other arithmetic  0.73 us (1%)
    pallas_call x1, Pallas kernels, on_device(): pl.pallas_call(functools.partial(kernel, per_dev, n_row, n_col), grid_spe...  62.4 us
    unnamed x1, local copies, waits for them, and re-layouts  2.31 us

profile of v3, /device:TPU:1, one launch (start us, length us, event | category | flops | bytes accessed | tf_op | source)
XLA Modules:
  0.0 66.2 jit_solution(2425002338968056917)
XLA Ops:
  0.0 0.7 %pad_add_fusion = s32[4,4,2]{1,2,0:T(2,128)S(1)} fusion(s32[1,4,2]{1,2,0:T(2,128)} %param.13, s32[1,4,2]{1,2,0:T(2,128)} %param.12, s32[1,4,2]{1,2,0:T(2,128)} %param.10, s32[1,4,2]{1,2,0:T(2,128)} %param.9), kind=kLoop, calls=%fused_computation | loop fusion | flops 96 | bytes 256 | tf_op jit(solution)/shard_map/concatenate | solution.py:434
  0.7 0.1 copy.9
  0.8 0.6 reshape.3.info
  1.5 62.4 %transport.1 = f32[256,1024]{1,0:T(8,128)} custom-call(s32[32]{0:T(128)} %reshape.3.info, f32[256,1024]{1,0:T(8,128)} %src.1, f32[1,4,512,512]{3,2,1,0:T(8,128)} %box_a.1, f32[1,4,512,512]{3,2,1,0:T(8,128)} %box_b.1), custom_call_target="tpu_custom_call" | custom-call | tf_op jit(solution)/shard_map/transport/pallas_call | solution.py:440
  63.9 2.3 %copy.11 = f32[256,1024]{1,0:T(8,128)} copy(f32[256,1024]{1,0:T(8,128)} %transport.1) | data formatting | bytes 2097152

commit v4 on v3

--- a/solution.py
+++ b/solution.py
@@ -86,9 +86,9 @@
 
 
 def units_of(per_dev):
-    units = [(per_dev - 2, 2 * per_dev, 3)]
-    units += [(j, 2 * j + 4, 2) for j in range(per_dev - 3, 0, -1)]
-    units += [(0, 2 * per_dev + 3, 1), (0, 0, 3), (0, 3, 3)]
+    units = [(per_dev - 2, 2 * per_dev, 4)]
+    units += [(j, 2 * j + 4, 2) for j in range(per_dev - 3, 1, -1)]
+    units += [(1, 5, 3), (0, 2 * per_dev + 4, 1), (0, 0, 3), (0, 3, 2)]
     return units
 
 
@@ -182,14 +182,12 @@
 
     def beside(k):
         if k == 0:
-            a, b, to = bl.at[OWN, cols : cols + 3 * LANES], cs.at[:, : 3 * LANES], at(0, 1)
-        elif k == 1:
-            a, b, to = bl.at[OWN, cols + 3 * LANES :], cs.at[:, 3 * LANES :], at(0, 1)
+            a, b, to = bl.at[OWN, cols:wide], cs, at(0, 1)
         else:
-            a, b, to = bl.at[OWN, cols + 3 * LANES :], cl, at(0, -1)
+            a, b, to = bl.at[OWN, wide:], cl, at(0, -1)
         return remote(a, b, c_send.at[k], c_recv.at[k], to)
 
-    sides = 2 if n_col == 2 else 3
+    sides = 2
 
     def hand_on(n):
         @pl.when(odd)
@@ -216,11 +214,12 @@
         else:
             near = canvas[:, lo:hi]
         res = dot_split(split(near), [b[: (count + 2) * LANES, : count * LANES] for b in (band_hi, band_lo)])
-        if first * LANES + count * LANES > wide:
-            bl[:, first * LANES :] = res[:, :LANES]
-            bl[:, :LANES] = res[:, LANES:]
-        else:
-            bl[:, tiles(first, count)] = res
+        bl[:, tiles(first, count)] = res
+
+    def smooth_edges(right_end):
+        near = jnp.concatenate([right_end, jnp.zeros((TALL, LANES), jnp.float32), canvas[:, :LANES]], axis=1)
+        band = [b[: 3 * LANES, :LANES] for b in (band_hi, band_lo)]
+        bl[:, wide:] = dot_split(split(near), band)
 
     def the_band():
         n = lax.broadcasted_iota(jnp.int32, (2 * S, S), 0)
@@ -358,7 +357,8 @@
             left = turned[t - 1] if t > 0 else zero
             right = turned[t] if t < BOX // LANES else zero
             spot = pl.ds(pl.multiple_of(j * S + t * LANES, LANES), LANES)
-            canvas[:, spot] += jnp.where(lane < s, left, right)
+            piece = jnp.where(lane < s, left, right)
+            canvas[:, spot] += piece
 
         for n, (when, first, count) in enumerate(units):
             if when > 0:
@@ -373,11 +373,11 @@
         def _():
             late = [n for n, u_ in enumerate(units) if u_[0] == 0]
             corner_unit, left_unit, right_unit = late
-            smooth(2 * per_dev + 3, 2)
+            smooth_edges(piece)
             give(corner_unit)
             mid = units[left_unit][2]
             last = units[right_unit][1] + units[right_unit][2]
-            for f in range(1, mid, 2):
+            for f in range(0, mid, 2):
                 smooth(f, min(2, mid - f))
             give(left_unit)
             hand_on(corner_unit)
@@ -400,10 +400,9 @@
             ln = lax.broadcasted_iota(jnp.int32, (S, LANES), 1)
             for k in range(sides):
                 beside(k).wait_recv()
-            out[:, : 3 * LANES] += cs[:, : 3 * LANES]
-            out[:, 3 * LANES : 4 * LANES] += jnp.where(ln < LANES - RADIUS, cs[:, 3 * LANES :], 0.0)
-            behind = cs[:, 3 * LANES :] if n_col == 2 else cl[...]
-            out[:, edge] += jnp.where(ln >= LANES - RADIUS, behind, 0.0)
+            out[:, : 4 * LANES] += cs[...]
+            out[:, tiles(5, 1)] += jnp.where(ln < RADIUS, bl[OWN, wide:], 0.0)
+            out[:, edge] += jnp.where(ln >= LANES - RADIUS, cl[...], 0.0)
 
             for k in range(3):
                 halo(src, mv_s, k, s_send, s_recv).wait_send()
@@ -454,12 +453,12 @@
                 f32(S, cols),
                 f32(S, cols),
                 f32(TALL, wide),
-                f32(TALL, wide),
+                f32(TALL, wide + LANES),
                 pltpu.VMEM((2 * S, S), jnp.bfloat16),
                 pltpu.VMEM((2 * S, S), jnp.bfloat16),
-                f32(S + DOWN2, wide),
-                f32(DOWN2, wide),
-                f32(RADIUS, wide),
+                f32(S + DOWN2, wide + LANES),
+                f32(DOWN2, wide + LANES),
+                f32(RADIUS, wide + LANES),
                 f32(S, 2 * S),
                 f32(S, LANES),
                 dma((3,)),

time: 66.4 us -> 68.5 us (1.032)
  Pallas kernels: 62.4 us -> 64.5 us
    pallas_call x1, Pallas kernels: 62.4 us -> 64.5 us  [on_device(): pl.pallas_call(functools.partial(kernel, per_dev, n_row, n_col), grid_spe...]
where the time goes in v4:
time: 68.5 us; the launch traced here: 68.3 us
  Pallas kernels  64.5 us (94%)
  local copies, waits for them, and re-layouts  3.03 us (4%)
  other arithmetic  0.73 us (1%)
    pallas_call x1, Pallas kernels, on_device(): pl.pallas_call(functools.partial(kernel, per_dev, n_row, n_col), grid_spe...  64.5 us
    unnamed x1, local copies, waits for them, and re-layouts  2.31 us

profile of v4, /device:TPU:1, one launch (start us, length us, event | category | flops | bytes accessed | tf_op | source)
XLA Modules:
  0.0 68.3 jit_solution(12176924041387754575)
XLA Ops:
  0.0 0.7 %pad_add_fusion = s32[4,4,2]{1,2,0:T(2,128)S(1)} fusion(s32[1,4,2]{1,2,0:T(2,128)} %param.13, s32[1,4,2]{1,2,0:T(2,128)} %param.12, s32[1,4,2]{1,2,0:T(2,128)} %param.10, s32[1,4,2]{1,2,0:T(2,128)} %param.9), kind=kLoop, calls=%fused_computation | loop fusion | flops 96 | bytes 256 | tf_op jit(solution)/shard_map/concatenate | solution.py:433
  0.7 0.1 copy.9
  0.8 0.6 reshape.3.info
  1.5 64.5 %transport.1 = f32[256,1024]{1,0:T(8,128)} custom-call(s32[32]{0:T(128)} %reshape.3.info, f32[256,1024]{1,0:T(8,128)} %src.1, f32[1,4,512,512]{3,2,1,0:T(8,128)} %box_a.1, f32[1,4,512,512]{3,2,1,0:T(8,128)} %box_b.1), custom_call_target="tpu_custom_call" | custom-call | tf_op jit(solution)/shard_map/transport/pallas_call | solution.py:439
  66.0 2.3 %copy.11 = f32[256,1024]{1,0:T(8,128)} copy(f32[256,1024]{1,0:T(8,128)} %transport.1) | data formatting | bytes 2097152
